TPU v7x, 256 devices: a whole 4x4x8 slice. The times are simulated.
256 devices in a mesh: dp: 16 (over x, y), tensor: 8 (over z), side: 2 (over core).
Axes of the slice: x: 4, y: 4, z: 8, core: 2. Of those that a mesh axis runs over, the one named last changes fastest.
Arguments:
- q_new: bfloat16 [1024, 6144], P(('dp', 'side'), 'tensor'), may hold values from -6 to 6
- k_new: bfloat16 [1024, 1024], P(('dp', 'side'), 'tensor'), may hold values from -6 to 6
- v_new: bfloat16 [1024, 1024], P(('dp', 'side'), 'tensor'), may hold values from -6 to 6
- k_cache: bfloat16 [1024, 192, 1024], P(('dp', 'side'), None, 'tensor'), may hold values from -6 to 6
- v_cache: bfloat16 [1024, 192, 1024], P(('dp', 'side'), None, 'tensor'), may hold values from -6 to 6
- lengths: int32 [1024], P(('dp', 'side')), may hold values from 24 to 192, as said below
- attn_out_weight: bfloat16 [6144, 6144], P('tensor', ('dp', 'side')), may hold values from -0.078125 to 0.078125
- residual: bfloat16 [1024, 6144], P('tensor', ('dp', 'side')), may hold values from -1.5 to 1.5
- norm_gain: float32 [6144], replicated, may hold values from 0.1 to 1.9
- router_weight: bfloat16 [6144, 8], replicated, may hold values from -0.02734375 to 0.02734375
- expert_ids: int32 [1024, 2], replicated, may hold values from 0 to 7, all different within a row; in each aligned block of 128 rows (0 to 127, 128 to 255, ...) at most 64 rows name the same one
- gate_weight: bfloat16 [8, 6144, 8192], P('tensor', None, ('dp', 'side')), may hold values from -0.078125 to 0.078125
- up_weight: bfloat16 [8, 6144, 8192], P('tensor', None, ('dp', 'side')), may hold values from -0.078125 to 0.078125
- down_weight: bfloat16 [8, 8192, 6144], P('tensor', ('dp', 'side')), may hold values from -0.0625 to 0.0625
Outputs:
- layer_out: bfloat16 [1024, 6144], P('tensor', ('dp', 'side'))
Inputs may be any that keep to these rules, and one draw needn't show every extreme that they name: `expert_ids`: each row names two different experts; in each aligned block of 128 rows no expert is named by more than 64 rows, and in every draw some expert is named by exactly 64 rows of a block. Row r attends to cached positions 0 to lengths[r] - 1 and to its new key; some rows hold all 192.
All inputs are finite; a program needn't handle non-finite values.
Results may differ from a plain program's by a relative error of at most 0.035.
Values may be sent and summed in bfloat16 or wider, within the bound.
No kernel may reach another device: no remote copies, remote signals or barrier semaphores. Data moves between devices by JAX's collectives and lax.ppermute only.
A program may use at most 128 MiB of HBM per device.

v0:
```python
import jax
import jax.numpy as jnp
from jax import lax
from jax.sharding import PartitionSpec as P

HEAD_DIM = 128
EXPERTS = 8
eps = 1e-05


def slot_tables(expert_ids, experts, blocks, most):
    rows = expert_ids.shape[0]
    block_rows = rows // blocks
    labels = jnp.arange(experts, dtype=jnp.int32)
    chosen = (expert_ids[:, :, None] == labels[None, None, :]).astype(jnp.int32)
    member = jnp.sum(chosen, axis=1)
    ranks = jnp.cumsum(member.reshape(blocks, block_rows, experts), axis=1)
    ranks = ranks.reshape(rows, experts) - 1
    block_of = jnp.arange(rows, dtype=jnp.int32) // block_rows
    slots = block_of[:, None] * most + ranks
    picked = jnp.sum(chosen * slots[:, None, :], axis=2)
    capacity = blocks * most
    row_ids = jnp.broadcast_to(jnp.arange(rows, dtype=jnp.int32)[:, None], (rows, 2))
    others = expert_ids[:, ::-1]
    leads = jnp.broadcast_to(jnp.array([1, 0], dtype=jnp.int32)[None, :], (rows, 2))
    table = jnp.full((experts, capacity), rows, jnp.int32).at[expert_ids, picked].set(row_ids)
    partner = jnp.zeros((experts, capacity), jnp.int32).at[expert_ids, picked].set(others)
    leading = jnp.zeros((experts, capacity), jnp.int32).at[expert_ids, picked].set(leads)
    return (picked, table, partner, leading)


def shards(
    q_new,
    k_new,
    v_new,
    k_cache,
    v_cache,
    lengths,
    attn_out_weight,
    residual,
    norm_gain,
    router_weight,
    expert_ids,
    gate_weight,
    up_weight,
    down_weight,
):
    rows_dev = q_new.shape[0]
    kv_local = k_new.shape[1] // HEAD_DIM
    heads_local = q_new.shape[1] // HEAD_DIM
    group_size = heads_local // kv_local
    cache_len = k_cache.shape[1]
    inv_root = HEAD_DIM ** (-0.5)
    queries = q_new.reshape(rows_dev, kv_local, group_size, HEAD_DIM)
    cache_keys = k_cache.reshape(rows_dev, cache_len, kv_local, HEAD_DIM)
    cache_values = v_cache.reshape(rows_dev, cache_len, kv_local, HEAD_DIM)
    own_keys = k_new.reshape(rows_dev, kv_local, HEAD_DIM)
    own_values = v_new.reshape(rows_dev, kv_local, HEAD_DIM).astype(jnp.float32)
    cache_scores = (
        jnp.einsum("rkgd,rckd->rkgc", queries, cache_keys, preferred_element_type=jnp.float32)
        * inv_root
    )
    own_scores = (
        jnp.einsum("rkgd,rkd->rkg", queries, own_keys, preferred_element_type=jnp.float32)
        * inv_root
    )
    live_mask = (jnp.arange(cache_len, dtype=jnp.int32)[None, :] < lengths[:, None])[
        :, None, None, :
    ]
    cache_scores = jnp.where(live_mask, cache_scores, -1e30)
    peak = jnp.maximum(jnp.max(cache_scores, axis=3), own_scores)
    cache_exp = jnp.exp(cache_scores - peak[..., None])
    own_exp = jnp.exp(own_scores - peak)
    denominator = jnp.sum(cache_exp, axis=3) + own_exp
    cache_weights = (cache_exp / denominator[..., None]).astype(jnp.bfloat16)
    own_weights = (own_exp / denominator).astype(jnp.bfloat16).astype(jnp.float32)
    mixed_heads = jnp.einsum(
        "rkgc,rckd->rkgd", cache_weights, cache_values, preferred_element_type=jnp.float32
    )
    mixed_heads = mixed_heads + own_weights[..., None] * own_values[:, :, None, :]
    attention = mixed_heads.reshape(rows_dev, heads_local * HEAD_DIM).astype(jnp.bfloat16)
    head_sums = jnp.dot(
        lax.all_gather(attention, ("dp", "side"), axis=0, tiled=True),
        attn_out_weight,
        preferred_element_type=jnp.float32,
    )
    total_rows = expert_ids.shape[0]
    tensor_count = lax.axis_size("tensor")
    tensor_rank = lax.axis_index("tensor")
    block_rows = total_rows // tensor_count
    most = block_rows // 2
    experts_local = gate_weight.shape[0]
    col_width = head_sums.shape[1]
    picked, table, partner, leading = slot_tables(expert_ids, EXPERTS, tensor_count, most)
    own_rows = lax.dynamic_slice_in_dim(
        head_sums, tensor_rank * block_rows, block_rows, 0
    ) + residual.astype(jnp.float32)
    head_sums = lax.dynamic_update_slice_in_dim(head_sums, own_rows, tensor_rank * block_rows, 0)
    routed = jnp.take(head_sums, table, axis=0, mode="fill", fill_value=0.0)
    hidden = lax.psum_scatter(
        routed.astype(jnp.bfloat16), "tensor", scatter_dimension=0, tiled=True
    )
    hidden_f = hidden.astype(jnp.float32)
    labels = jnp.arange(EXPERTS, dtype=jnp.int32)
    mine = tensor_rank * experts_local + jnp.arange(experts_local, dtype=jnp.int32)
    features = lax.all_gather(hidden, ("dp", "side"), axis=2, tiled=True).astype(jnp.float32)
    normed = (
        features * lax.rsqrt(jnp.mean(features * features, axis=2, keepdims=True) + eps) * norm_gain
    ).astype(jnp.bfloat16)
    gate = jnp.einsum("ecd,edf->ecf", normed, gate_weight, preferred_element_type=jnp.float32)
    upward = jnp.einsum("ecd,edf->ecf", normed, up_weight, preferred_element_type=jnp.float32)
    logits = jnp.einsum("ecd,dk->eck", normed, router_weight, preferred_element_type=jnp.float32)
    inner = (jax.nn.silu(gate) * upward).astype(jnp.bfloat16)
    summed = lax.psum_scatter(
        jnp.einsum("efd,ecf->dec", down_weight, inner, preferred_element_type=jnp.float32).astype(
            jnp.bfloat16
        ),
        ("dp", "side"),
        scatter_dimension=0,
        tiled=True,
    ).astype(jnp.float32)
    expert_out = jnp.transpose(summed, (1, 2, 0))
    own_logit = jnp.sum(jnp.where(mine[:, None, None] == labels, logits, 0.0), axis=2)
    partner_mine = lax.dynamic_slice_in_dim(partner, tensor_rank * experts_local, experts_local, 0)
    other_logit = jnp.sum(jnp.where(partner_mine[..., None] == labels, logits, 0.0), axis=2)
    shares = jax.nn.sigmoid(own_logit - other_logit)
    parts = (shares[..., None] * expert_out).astype(jnp.bfloat16)
    table_mine = lax.dynamic_slice_in_dim(table, tensor_rank * experts_local, experts_local, 0)
    leading_mine = lax.dynamic_slice_in_dim(leading, tensor_rank * experts_local, experts_local, 0)
    values = parts.astype(jnp.float32) + hidden_f * leading_mine[..., None].astype(jnp.float32)
    buffer = (
        jnp.zeros((total_rows, col_width), jnp.float32)
        .at[table_mine.reshape(-1)]
        .add(values.reshape(-1, col_width), mode="drop")
    )
    out_rows = lax.psum_scatter(
        buffer.astype(jnp.bfloat16), "tensor", scatter_dimension=0, tiled=True
    )
    return out_rows


def solution(mesh):
    return jax.shard_map(
        shards,
        mesh=mesh,
        in_specs=(
            P(("dp", "side"), "tensor"),
            P(("dp", "side"), "tensor"),
            P(("dp", "side"), "tensor"),
            P(("dp", "side"), None, "tensor"),
            P(("dp", "side"), None, "tensor"),
            P(("dp", "side")),
            P("tensor", ("dp", "side")),
            P("tensor", ("dp", "side")),
            P(),
            P(),
            P(),
            P("tensor", None, ("dp", "side")),
            P("tensor", None, ("dp", "side")),
            P("tensor", ("dp", "side"), None),
        ),
        out_specs=P("tensor", ("dp", "side")),
        check_vma=False,
    )
```

profile of v0, /device:TPU:2, one launch (start us, length us, event | category | flops | bytes accessed | tf_op | source)
XLA Modules:
  0.0 374.5 jit_solution(10705472872214771290)
XLA Ops:
  6.5 0.9 iota_compare_fusion.1
  7.4 0.8 convert_element_type.84
  8.2 0.9 reshape.270
  9.1 0.9 fusion.27
  9.9 0.0 copy-start.11
  10.0 0.0 copy-start.12
  10.0 2.4 fusion.44
  12.4 0.2 fusion.24
  12.6 0.0 copy-start.4
  12.6 2.0 fusion.17
  14.7 0.6 copy.56
  15.3 0.0 all-gather.3.cloned.1.call-update
  15.3 0.0 reduce-scatter.6.cloned.1.call-start
  15.4 0.0 copy-done.5
  15.4 1.0 copy.36
  16.4 2.0 broadcast_add_fusion
  18.4 1.2 copy.37
  19.7 0.1 multiply_reduce_fusion
  19.8 0.1 and_reduce_fusion
  19.9 1.0 copy.38
  21.0 1.3 reshape.304
  22.3 0.8 broadcast_in_dim.46
  23.1 1.3 reshape.306
  24.4 8.1 %scatter_custom_fusion.1 = s32[4096]{0:T(1024)S(1)} fusion(s32[2048]{0:T(1024)S(1)} %reshape.304, s32[2048]{0:T(1024)S(1)} %reshape.306, s32[]{:T(128)} %constant.27.clone.1), kind=kCustom, calls=%fused_computation.68 | custom fusion | bytes 16388
  32.6 33.8 %all-gather.3.cloned.1.call-done = bf16[1024,768]{1,0:T(8,128)(2,1)} async-done(((bf16[32,768]{1,0:T(8,128)(2,1)}), bf16[1024,768]{1,0:T(8,128)(2,1)}) %all-gather.3.cloned.1.call-update) | async-done | bytes 1572880 | tf_op jit(solution)/shard_map/all_gather | solution.py:83
  66.4 3.0 fusion.45
  69.3 1.6 add_dynamic-update-slice_fusion
  70.9 2.1 copy.39
  73.0 16.9 %gather_fusion = bf16[4096,192]{1,0:T(8,128)(2,1)} fusion(bf16[1024,192]{1,0:T(8,128)(2,1)} %copy.39, s32[4096]{0:T(1024)S(1)} %broadcast_clamp_fusion), kind=kCustom, calls=%fused_computation | custom fusion | bytes 3162112 | tf_op jit(solution)/shard_map/jit(_take)/gather | solution.py:99
  90.0 3.8 %copy.40 = bf16[8,512,192]{1,2,0:T(8,128)(2,1)} copy(bf16[8,512,192]{2,1,0:T(8,128)(2,1)} %bitcast.68) | data formatting | bytes 3145728 | tf_op jit(solution)/shard_map/jit(_take)/gather | solution.py:99
  93.8 2.9 select_convert_fusion
  96.7 0.0 reduce-scatter.6.cloned.1.call-update
  96.7 0.0 all-gather.5.cloned.1.call-start
  96.8 40.2 %reduce-scatter.6.cloned.1.call-done = bf16[1,512,192]{1,2,0:T(8,128)(2,1)} async-done(((bf16[8,512,192]{1,2,0:T(8,128)(2,1)}), bf16[1,512,192]{1,2,0:T(8,128)(2,1)}) %reduce-scatter.6.cloned.1.call-update) | async-done | bytes 196624 | tf_op jit(solution)/shard_map/reduce_scatter | solution.py:100
  137.0 0.0 all-gather.5.cloned.1.call-update
  137.0 0.2 reduce-scatter.10.cloned.1.call-start
  137.2 54.3 %all-gather.5.cloned.1.call-done = bf16[1,512,6144]{1,2,0:T(8,128)(2,1)} async-done(((bf16[1,512,192]{1,2,0:T(8,128)(2,1)}), bf16[1,512,6144]{1,2,0:T(8,128)(2,1)}) %all-gather.5.cloned.1.call-update) | async-done | bytes 6291472 | tf_op jit(solution)/shard_map/all_gather | solution.py:106
  191.6 4.3 %fusion = f32[512]{0:T(512)S(1)} fusion(bf16[1,512,6144]{1,2,0:T(8,128)(2,1)} %all-gather.5.cloned.1.call-done), kind=kLoop, calls=%fused_computation.7 | loop fusion | flops 9436672 | bytes 6293504 | tf_op jit(solution)/shard_map/reduce_sum | solution.py:108
  195.9 0.3 copy-done.2
  196.2 1.6 fusion.4
  197.8 2.7 copy-done.1
  200.4 2.6 fusion.8
  203.1 13.1 %fusion.3 = bf16[6144,512]{0,1:T(8,128)(2,1)} fusion(bf16[1,256,6144]{2,1,0:T(8,128)(2,1)S(1)} %copy-done, bf16[512,6144]{0,1:T(8,128)(2,1)} %copy-done.1, bf16[1,6144,256]{2,1,0:T(8,128)(2,1)} %param.27, f32[512,256]{1,0:T(8,128)} %fusion.8), kind=kOutput, calls=%fused_computation.11 | convolution fusion | flops 3225157632 | bytes 19398656 | tf_op jit(solution)/shard_map/efd,ecf->dec/dot_general | solution.py:115
  216.1 8.6 %copy.49 = bf16[6144,512]{1,0:T(8,128)(2,1)} copy(bf16[6144,512]{0,1:T(8,128)(2,1)} %fusion.3) | data formatting | bytes 12582912
  224.8 0.0 reduce-scatter.10.cloned.1.call-update
  224.8 0.0 reduce-scatter.8.cloned.1.call-start
  224.8 0.2 rev.3
  225.1 1.1 copy.41
  226.1 1.3 reshape.312
  227.4 8.4 %scatter_custom_fusion.2 = s32[4096]{0:T(1024)S(1)} fusion(s32[2048]{0:T(1024)} %copy-done.9, s32[2048]{0:T(1024)S(1)} %reshape.312, s32[]{:T(128)} %constant.28.clone.1), kind=kCustom, calls=%fused_computation.66 | custom fusion | bytes 16896
  235.9 0.9 broadcast_in_dim.94
  236.7 1.3 reshape.318
  238.1 8.2 %scatter_custom_fusion.3 = s32[4096]{0:T(1024)S(1)} fusion(s32[2048]{0:T(1024)} %copy-done.9, s32[2048]{0:T(1024)S(1)} %reshape.318, s32[]{:T(128)} %constant.28.clone.1), kind=kCustom, calls=%fused_computation.64 | custom fusion | bytes 16896
  246.4 4.0 %select_reduce_fusion.1 = (f32[512]{0:T(512)S(1)}, f32[512]{0:T(512)S(1)}) fusion(s32[512]{0:T(512)S(1)} %bitcast.76, pred[8]{0:T(512)(128)(4,1)S(1)} %iota_compare_fusion.3, bf16[512,6144]{0,1:T(8,128)(2,1)} %copy-done.1, bf16[6144,8]{0,1:T(8,128)(2,1)S(1)} %copy-done.6), kind=kOutput, calls=%fused_computation.50 | convolution fusion | flops 50351104 | bytes 6395912 | tf_op jit(solution)/shard_map/ecd,dk->eck/dot_general | solution.py:112
  250.4 68.0 %reduce-scatter.10.cloned.1.call-done = bf16[192,512]{1,0:T(8,128)(2,1)} async-done(((bf16[6144,512]{1,0:T(8,128)(2,1)}), bf16[192,512]{1,0:T(8,128)(2,1)}) %reduce-scatter.10.cloned.1.call-update) | async-done | bytes 196624
  318.4 1.1 copy.50
  319.4 0.8 copy.42
  320.2 1.1 fusion.22
  321.3 1.0 copy.43
  322.3 4.8 %scatter_custom_fusion = f32[1024,192]{1,0:T(8,128)} fusion(s32[512]{0:T(512)S(1)} %bitcast.78, f32[512,192]{1,0:T(8,128)} %copy.43, f32[]{:T(128)} %constant.25.clone.1), kind=kCustom, calls=%fused_computation.25 | custom fusion | flops 98304 | bytes 786944 | tf_op jit(solution)/shard_map/scatter-add | solution.py:134
  327.1 2.1 convert_element_type.102
  329.2 0.0 reduce-scatter.8.cloned.1.call-update
  329.3 37.1 %reduce-scatter.8.cloned.1.call-done = bf16[128,192]{1,0:T(8,128)(2,1)} async-done(((bf16[1024,192]{1,0:T(8,128)(2,1)}), bf16[128,192]{1,0:T(8,128)(2,1)}) %reduce-scatter.8.cloned.1.call-update) | async-done | bytes 49168 | tf_op jit(solution)/shard_map/reduce_scatter | solution.py:136
  366.4 1.6 copy.44
  (43 shorter events, 0.2 us)
Async XLA Ops:
  6.5 196.5 %copy-start = (bf16[1,256,6144]{2,1,0:T(8,128)(2,1)S(1)}, bf16[1,256,6144]{2,1,0:T(8,128)(2,1)}, u32[]{:S(2)}) copy-start(bf16[1,256,6144]{2,1,0:T(8,128)(2,1)} %param.28) | copy-start | bytes 9437188
  6.5 8.8 %copy-start.5 = (s32[1024,2]{0,1:T(2,128)S(1)}, s32[1024,2]{0,1:T(2,128)}, u32[]{:S(2)}) copy-start(s32[1024,2]{0,1:T(2,128)} %param.25) | copy-start | bytes 24580
  6.5 59.8 %all-gather.3.cloned.1.call-start = ((), (), s32[]{:S(2)}) async-start(), calls=%async_computation.3 | async-start | bytes 1622016 | tf_op jit(solution)/shard_map/all_gather | solution.py:83
  9.9 9.8 %copy-start.11 = (s32[2]{0:T(128)S(1)}, s32[2]{0:T(128)}, u32[]{:S(2)}) copy-start(s32[2]{0:T(128)} %constant.84) | copy-start | bytes 28
  10.0 9.8 %copy-start.12 = (s32[2]{0:T(128)S(1)}, s32[2]{0:T(128)}, u32[]{:S(2)}) copy-start(s32[2]{0:T(128)} %constant.87) | copy-start | bytes 28
  12.6 53.7 %copy-start.4 = (bf16[768,192]{0,1:T(8,128)(2,1)S(1)}, bf16[768,192]{0,1:T(8,128)(2,1)}, u32[]{:S(2)}) copy-start(bf16[768,192]{0,1:T(8,128)(2,1)} %param.21) | copy-start | bytes 884740
  15.3 121.6 %reduce-scatter.6.cloned.1.call-start = ((), (), s32[]{:S(2)}) async-start(), calls=%async_computation.4 | async-start | bytes 1769472 | tf_op jit(solution)/shard_map/reduce_scatter | solution.py:100
  16.4 52.9 %copy-start.7 = (bf16[128,192]{0,1:T(8,128)(2,1)S(1)}, bf16[128,192]{0,1:T(8,128)(2,1)}, u32[]{:S(2)}) copy-start(bf16[128,192]{0,1:T(8,128)(2,1)} %param.22) | copy-start | bytes 147460
  22.3 2.2 copy-start.9
  96.7 94.8 %all-gather.5.cloned.1.call-start = ((), (), s32[]{:S(2)}) async-start(), calls=%async_computation.5 | async-start | bytes 6488064 | tf_op jit(solution)/shard_map/all_gather | solution.py:106
  137.0 58.9 %copy-start.8 = (f32[6144]{0:T(1024)S(1)}, f32[6144]{0:T(1024)}, u32[]{:S(2)}) copy-start(f32[6144]{0:T(1024)} %param.23) | copy-start | bytes 73732
  137.0 181.4 %reduce-scatter.10.cloned.1.call-start = ((), (), s32[]{:S(2)}) async-start(), calls=%async_computation.7 | async-start | bytes 6488064
  191.6 4.6 %copy-start.2 = (bf16[1,512,6144]{1,2,0:T(8,128)(2,1)S(1)}, bf16[1,512,6144]{1,2,0:T(8,128)(2,1)}, u32[]{:S(2)}) copy-start(bf16[1,512,6144]{1,2,0:T(8,128)(2,1)} %all-gather.5.cloned.1.call-done) | copy-start | bytes 18874372
  196.2 4.3 %copy-start.3 = (bf16[1,6144,256]{2,1,0:T(8,128)(2,1)S(1)}, bf16[1,6144,256]{2,1,0:T(8,128)(2,1)}, u32[]{:S(2)}) copy-start(bf16[1,6144,256]{2,1,0:T(8,128)(2,1)} %param.26) | copy-start | bytes 9437188
  197.8 2.7 copy-start.1
  224.8 11.1 %copy-start.10 = (s32[2]{0:T(128)S(1)}, s32[2]{0:T(128)}, u32[]{:S(2)}) copy-start(s32[2]{0:T(128)} %constant.80.clone) | copy-start | bytes 28
  224.8 21.6 %copy-start.6 = (bf16[6144,8]{0,1:T(8,128)(2,1)S(1)}, bf16[6144,8]{0,1:T(8,128)(2,1)}, u32[]{:S(2)}) copy-start(bf16[6144,8]{0,1:T(8,128)(2,1)} %param.24) | copy-start | bytes 294916
  224.8 141.6 %reduce-scatter.8.cloned.1.call-start = ((), (), s32[]{:S(2)}) async-start(), calls=%async_computation.6 | async-start | bytes 589824 | tf_op jit(solution)/shard_map/reduce_scatter | solution.py:136
Sparse Core Ops, SparseCore 0:
  15.4 50.8 all-gather.2
  96.8 40.0 reduce-scatter.5
  139.5 51.9 all-gather.4
  224.9 93.4 reduce-scatter.9
  329.4 36.9 reduce-scatter.7
where the time goes:
time: 376 us; the launch traced here: 374 us
  waiting for transfers between devices  234 us (62%)
  local copies, waits for them, and re-layouts  76.7 us (20%)
  matrix products  27.9 us (7%)
  other arithmetic  22.5 us (6%)
  between operations  13.5 us (4%)
    unnamed x6, waiting for transfers between devices  68.1 us
    all_gather x1, waiting for transfers between devices, shards(): lax.all_gather(hidden, ('dp', 'side'), axis=2, tiled=True)  54.3 us
    unnamed x35, local copies, waits for them, and re-layouts  40.4 us
    reduce_scatter x1, waiting for transfers between devices, shards(): lax.psum_scatter(routed.astype(jnp.bfloat16), 'tensor', scatter_dimension...  40.2 us
    reduce_scatter x1, waiting for transfers between devices, shards(): lax.psum_scatter(buffer.astype(jnp.bfloat16), 'tensor', scatter_dimension...  37.1 us
    all_gather x1, waiting for transfers between devices, shards(): lax.all_gather(attention, ('dp', 'side'), axis=0, tiled=True)  33.8 us
    gather x2, local copies, waits for them, and re-layouts, shards(): routed = jnp.take(head_sums, table, axis=0, mode='fill', fill_value=0.0)  20.8 us
    dot_general x1, matrix products, shards(): jnp.einsum('efd,ecf->dec', down_weight, inner, preferred_element_type=jnp...  13.1 us
  transfers between devices with their start and end apart: 5, of which 5 were waited for; matrix products, arithmetic and copies ran while one was open for 11% of the time, Pallas kernels for 0%

commit v1 on v0

--- a/solution.py
+++ b/solution.py
@@ -103,7 +103,10 @@
     hidden_f = hidden.astype(jnp.float32)
     labels = jnp.arange(EXPERTS, dtype=jnp.int32)
     mine = tensor_rank * experts_local + jnp.arange(experts_local, dtype=jnp.int32)
-    features = lax.all_gather(hidden, ("dp", "side"), axis=2, tiled=True).astype(jnp.float32)
+    features = jnp.concatenate(
+        lax.all_to_all(jnp.stack([hidden] * lax.axis_size(("dp", "side"))), ("dp", "side"), 0, 0),
+        axis=2,
+    ).astype(jnp.float32)
     normed = (
         features * lax.rsqrt(jnp.mean(features * features, axis=2, keepdims=True) + eps) * norm_gain
     ).astype(jnp.bfloat16)

time: 376 us -> 416 us (1.11)
  waiting for transfers between devices: 234 us -> 265 us
  other arithmetic: 22.5 us -> 31.4 us
  starting transfers between devices: 0.35 us -> 7.93 us
  local copies, waits for them, and re-layouts: 76.7 us -> 72 us
    all_to_all x0 -> x1, waiting for transfers between devices: none -> 76.6 us  [shards(): lax.all_to_all(jnp.stack([hidden] * lax.axis_size(('dp', 'side'))), ('dp'...]
    all_gather x1 -> x0, waiting for transfers between devices: 54.3 us -> none  [shards(): lax.all_gather(hidden, ('dp', 'side'), axis=2, tiled=True)]
    unnamed x6 -> x5, waiting for transfers between devices: 68.1 us -> 76.3 us
    all_to_all x0 -> x1, starting transfers between devices: none -> 7.59 us  [shards(): lax.all_to_all(jnp.stack([hidden] * lax.axis_size(('dp', 'side'))), ('dp'...]
    convert_element_type x0 -> x2, other arithmetic: none -> 6.08 us  [the longest x1 4.66 us: shards(): features = jnp.concatenate(lax.all_to_all(jnp.stack([hidden] * lax.axis_s...]
    gather x2 -> x1, local copies, waits for them, and re-layouts: 20.8 us -> 16.9 us  [shards(): routed = jnp.take(head_sums, table, axis=0, mode='fill', fill_value=0.0)]
    unnamed x35 -> x33, local copies, waits for them, and re-layouts: 40.4 us -> 40.5 us
  transfers between devices with their start and end apart: 5 -> 5, of which waited for: 5 -> 5; matrix products, arithmetic and copies ran while one was open for 11% -> 10% of each run, Pallas kernels for 0% -> 0%
where the time goes in v1:
time: 416 us; the launch traced here: 415 us
  waiting for transfers between devices  265 us (64%)
  local copies, waits for them, and re-layouts  72 us (17%)
  other arithmetic  31.4 us (8%)
  matrix products  24.8 us (6%)
  between operations  13.5 us (3%)
  starting transfers between devices  7.93 us (2%)
    all_to_all x1, waiting for transfers between devices, shards(): lax.all_to_all(jnp.stack([hidden] * lax.axis_size(('dp', 'side'))), ('dp'...  76.6 us
    unnamed x5, waiting for transfers between devices  76.3 us
    reduce_scatter x1, waiting for transfers between devices, shards(): lax.psum_scatter(routed.astype(jnp.bfloat16), 'tensor', scatter_dimension...  41.9 us
    unnamed x33, local copies, waits for them, and re-layouts  40.5 us
    reduce_scatter x1, waiting for transfers between devices, shards(): lax.psum_scatter(buffer.astype(jnp.bfloat16), 'tensor', scatter_dimension...  37.1 us
    all_gather x1, waiting for transfers between devices, shards(): lax.all_gather(attention, ('dp', 'side'), axis=0, tiled=True)  33.1 us
    gather x1, local copies, waits for them, and re-layouts, shards(): routed = jnp.take(head_sums, table, axis=0, mode='fill', fill_value=0.0)  16.9 us
    dot_general x1, matrix products, shards(): jnp.einsum('efd,ecf->dec', down_weight, inner, preferred_element_type=jnp...  13.1 us
  transfers between devices with their start and end apart: 5, of which 5 were waited for; matrix products, arithmetic and copies ran while one was open for 10% of the time, Pallas kernels for 0%

profile of v1, /device:TPU:2, one launch (start us, length us, event | category | flops | bytes accessed | tf_op | source)
XLA Modules:
  0.0 414.7 jit_solution(7036965382826637167)
XLA Ops:
  6.5 0.0 copy-start
  6.5 0.0 all-gather.2.cloned.1.call-start
  6.6 0.9 iota_compare_fusion.1
  7.5 0.9 convert_element_type.115
  8.3 0.9 reshape.339
  9.2 0.9 fusion.31
  10.1 2.4 fusion.48
  12.5 0.2 fusion.28
  12.7 2.0 fusion.15
  14.7 0.6 copy.55
  15.3 0.0 all-gather.2.cloned.1.call-update
  15.4 0.0 reduce-scatter.6.cloned.1.call-start
  15.4 0.7 convert_reduce_fusion
  16.1 1.0 copy.36
  17.1 2.0 broadcast_add_fusion
  19.1 1.2 copy.37
  20.4 0.1 multiply_reduce_fusion.1
  20.5 0.1 and_reduce_fusion
  20.6 1.0 copy.38
  21.7 1.3 reshape.373
  23.0 0.8 broadcast_in_dim.46
  23.8 1.3 reshape.375
  25.1 8.1 %scatter_custom_fusion.1 = s32[4096]{0:T(1024)S(1)} fusion(s32[2048]{0:T(1024)S(1)} %reshape.373, s32[2048]{0:T(1024)S(1)} %reshape.375, s32[]{:T(128)} %constant.27.clone.1), kind=kCustom, calls=%fused_computation.74 | custom fusion | bytes 16388
  33.3 33.1 %all-gather.2.cloned.1.call-done = bf16[1024,768]{1,0:T(8,128)(2,1)} async-done(((bf16[32,768]{1,0:T(8,128)(2,1)}), bf16[1024,768]{1,0:T(8,128)(2,1)}) %all-gather.2.cloned.1.call-update) | async-done | bytes 1572880 | tf_op jit(solution)/shard_map/all_gather | solution.py:83
  66.4 3.0 fusion.49
  69.4 1.6 add_dynamic-update-slice_fusion
  70.9 2.1 copy.39
  73.1 16.9 %gather_fusion = bf16[4096,192]{1,0:T(8,128)(2,1)} fusion(bf16[1024,192]{1,0:T(8,128)(2,1)} %copy.39, s32[4096]{0:T(1024)S(1)} %broadcast_clamp_fusion), kind=kCustom, calls=%fused_computation | custom fusion | bytes 3162112 | tf_op jit(solution)/shard_map/jit(_take)/gather | solution.py:99
  90.0 2.9 select_convert_fusion
  92.9 0.0 reduce-scatter.6.cloned.1.call-update
  92.9 41.9 %reduce-scatter.6.cloned.1.call-done = bf16[1,512,192]{2,1,0:T(8,128)(2,1)} async-done(((bf16[8,512,192]{2,1,0:T(8,128)(2,1)}), bf16[1,512,192]{2,1,0:T(8,128)(2,1)}) %reduce-scatter.6.cloned.1.call-update) | async-done | bytes 196624 | tf_op jit(solution)/shard_map/reduce_scatter | solution.py:100
  134.9 1.1 copy.40
  135.9 3.4 stack.2
  139.3 7.6 %all-to-all-start = ((bf16[32,1,512,192]{2,3,1,0:T(8,128)(2,1)}), bf16[32,1,512,192]{2,3,1,0:T(8,128)(2,1)}, u32[]{:S(2)}, u32[]{:S(2)}) async-start(bf16[32,1,512,192]{2,3,1,0:T(8,128)(2,1)} %stack.2), calls=%async_computation.1 | async-start | bytes 12582912 | tf_op jit(solution)/shard_map/all_to_all | solution.py:107
  146.9 0.2 reduce-scatter.10.cloned.1.call-start
  147.1 0.1 mul.152
  147.2 76.6 %all-to-all-done = bf16[32,1,512,192]{2,3,1,0:T(8,128)(2,1)} async-done(((bf16[32,1,512,192]{2,3,1,0:T(8,128)(2,1)}), bf16[32,1,512,192]{2,3,1,0:T(8,128)(2,1)}, u32[]{:S(2)}, u32[]{:S(2)}) %all-to-all-start) | async-done | bytes 6291488 | tf_op jit(solution)/shard_map/all_to_all | solution.py:107
  223.8 4.4 %multiply_reduce_fusion = f32[512]{0:T(512)S(1)} fusion(bf16[32,1,512,192]{2,3,1,0:T(8,128)(2,1)} %all-to-all-done), kind=kLoop, calls=%fused_computation.9 | loop fusion | flops 9436672 | bytes 6293504 | tf_op jit(solution)/shard_map/reduce_sum | solution.py:111
  228.3 4.5 %multiply_convert_fusion = bf16[32,1,512,192]{2,3,0,1:T(8,128)(2,1)S(1)} fusion(bf16[32,1,512,192]{2,3,1,0:T(8,128)(2,1)} %all-to-all-done, f32[32,192]{1,0:T(8,128)S(1)} %mul.152, f32[512]{0:T(512)S(1)} %add_rsqrt_fusion), kind=kLoop, calls=%fused_computation.8 | loop fusion | flops 12582912 | bytes 12609536 | tf_op jit(solution)/shard_map/convert.3
  232.8 2.6 copy-done.2
  235.4 2.6 fusion.6
  238.0 0.0 copy-done
  238.0 13.1 %fusion.2 = bf16[6144,512]{0,1:T(8,128)(2,1)} fusion(bf16[1,256,6144]{2,1,0:T(8,128)(2,1)S(1)} %copy-done, bf16[512,6144]{0,1:T(8,128)(2,1)} %bitcast.91, bf16[1,6144,256]{2,1,0:T(8,128)(2,1)} %param.27, f32[512,256]{1,0:T(8,128)} %fusion.6), kind=kOutput, calls=%fused_computation.11 | convolution fusion | flops 3225157632 | bytes 19398656 | tf_op jit(solution)/shard_map/efd,ecf->dec/dot_general | solution.py:118
  251.1 8.7 %copy.48 = bf16[6144,512]{1,0:T(8,128)(2,1)} copy(bf16[6144,512]{0,1:T(8,128)(2,1)} %fusion.2) | data formatting | bytes 12582912
  259.8 0.0 reduce-scatter.10.cloned.1.call-update
  259.9 0.0 reduce-scatter.8.cloned.1.call-start
  259.9 0.2 rev.3
  260.1 0.2 copy.42
  260.4 0.3 reshape.381
  260.6 8.3 %scatter_custom_fusion.2 = s32[4096]{0:T(1024)S(1)} fusion(s32[2048]{0:T(1024)S(1)} %reshape.373, s32[2048]{0:T(1024)S(1)} %reshape.381, s32[]{:T(128)} %constant.28.clone.1), kind=kCustom, calls=%fused_computation.72 | custom fusion | bytes 16388
  269.0 0.3 reshape.387
  269.3 8.1 %scatter_custom_fusion.3 = s32[4096]{0:T(1024)S(1)} fusion(s32[2048]{0:T(1024)S(1)} %reshape.373, s32[2048]{0:T(1024)S(1)} %reshape.387, s32[]{:T(128)} %constant.28.clone.1), kind=kCustom, calls=%fused_computation.70 | custom fusion | bytes 16388
  277.4 4.7 %bitcast_convert_fusion = f32[32,1,512,192]{2,3,0,1:T(8,128)S(1)} fusion(bf16[32,1,512,192]{2,3,1,0:T(8,128)(2,1)} %all-to-all-done), kind=kLoop, calls=%fused_computation.12 | loop fusion | flops 3145728 | bytes 18874368 | tf_op jit(solution)/shard_map/convert_element_type | solution.py:109
  282.1 0.0 copy-start.7
  282.1 0.0 copy-start.1
  282.1 1.4 fusion.1
  283.5 0.9 select_reduce_fusion.1
  284.5 76.2 %reduce-scatter.10.cloned.1.call-done = bf16[192,512]{1,0:T(8,128)(2,1)} async-done(((bf16[6144,512]{1,0:T(8,128)(2,1)}), bf16[192,512]{1,0:T(8,128)(2,1)}) %reduce-scatter.10.cloned.1.call-update) | async-done | bytes 196624
  360.7 1.8 copy.49
  362.5 4.9 %scatter_custom_fusion = f32[1024,192]{1,0:T(8,128)} fusion(s32[512]{0:T(512)S(1)} %bitcast.102, bf16[1,512,192]{2,1,0:T(8,128)(2,1)S(1)} %copy-done.4, f32[]{:T(128)} %constant.25.clone.1, bf16[192,512]{0,1:T(8,128)(2,1)} %copy.49, f32[512]{0:T(512)S(1)} %bitcast.101, f32[512]{0:T(512)S(1)} %add_divide_fusion), kind=kCustom, calls=%fused_computation.25 | custom fusion | flops 786432 | bytes 1249284 | tf_op jit(solution)/shard_map/scatter-add | solution.py:137
  367.4 2.1 convert_element_type.137
  369.5 0.0 reduce-scatter.8.cloned.1.call-update
  369.5 37.1 %reduce-scatter.8.cloned.1.call-done = bf16[128,192]{1,0:T(8,128)(2,1)} async-done(((bf16[1024,192]{1,0:T(8,128)(2,1)}), bf16[128,192]{1,0:T(8,128)(2,1)}) %reduce-scatter.8.cloned.1.call-update) | async-done | bytes 49168 | tf_op jit(solution)/shard_map/reduce_scatter | solution.py:139
  406.6 1.6 copy.43
  (41 shorter events, 0.3 us)
Async XLA Ops:
  6.5 231.5 %copy-start = (bf16[1,256,6144]{2,1,0:T(8,128)(2,1)S(1)}, bf16[1,256,6144]{2,1,0:T(8,128)(2,1)}, u32[]{:S(2)}) copy-start(bf16[1,256,6144]{2,1,0:T(8,128)(2,1)} %param.28) | copy-start | bytes 9437188
  6.5 13.9 %copy-start.10 = (s32[2]{0:T(128)S(1)}, s32[2]{0:T(128)}, u32[]{:S(2)}) copy-start(s32[2]{0:T(128)} %constant.84) | copy-start | bytes 28
  6.5 14.0 %copy-start.11 = (s32[2]{0:T(128)S(1)}, s32[2]{0:T(128)}, u32[]{:S(2)}) copy-start(s32[2]{0:T(128)} %constant.87) | copy-start | bytes 28
  6.5 13.8 %copy-start.6 = (s32[1024,2]{0,1:T(2,128)S(1)}, s32[1024,2]{0,1:T(2,128)}, u32[]{:S(2)}) copy-start(s32[1024,2]{0,1:T(2,128)} %param.25) | copy-start | bytes 24580
  6.5 59.9 %copy-start.5 = (bf16[768,192]{0,1:T(8,128)(2,1)S(1)}, bf16[768,192]{0,1:T(8,128)(2,1)}, u32[]{:S(2)}) copy-start(bf16[768,192]{0,1:T(8,128)(2,1)} %param.21) | copy-start | bytes 884740
  6.5 59.9 %all-gather.2.cloned.1.call-start = ((), (), s32[]{:S(2)}) async-start(), calls=%async_computation.4 | async-start | bytes 1622016 | tf_op jit(solution)/shard_map/all_gather | solution.py:83
  15.4 119.5 %reduce-scatter.6.cloned.1.call-start = ((), (), s32[]{:S(2)}) async-start(), calls=%async_computation.5 | async-start | bytes 2359296 | tf_op jit(solution)/shard_map/reduce_scatter | solution.py:100
  139.3 7.8 %copy-start.8 = (f32[6144]{0:T(1024)S(1)}, f32[6144]{0:T(1024)}, u32[]{:S(2)}) copy-start(f32[6144]{0:T(1024)} %param.23) | copy-start | bytes 73732
  139.3 84.5 %all-to-all-start = ((bf16[32,1,512,192]{2,3,1,0:T(8,128)(2,1)}), bf16[32,1,512,192]{2,3,1,0:T(8,128)(2,1)}, u32[]{:S(2)}, u32[]{:S(2)}) async-start(bf16[32,1,512,192]{2,3,1,0:T(8,128)(2,1)} %stack.2), calls=%async_computation.1 | async-start | bytes 12582912 | tf_op jit(solution)/shard_map/all_to_all | solution.py:107
  146.9 213.8 %reduce-scatter.10.cloned.1.call-start = ((), (), s32[]{:S(2)}) async-start(), calls=%async_computation.7 | async-start | bytes 6488064
  228.3 7.1 %copy-start.3 = (bf16[1,6144,256]{2,1,0:T(8,128)(2,1)S(1)}, bf16[1,6144,256]{2,1,0:T(8,128)(2,1)}, u32[]{:S(2)}) copy-start(bf16[1,6144,256]{2,1,0:T(8,128)(2,1)} %param.26) | copy-start | bytes 9437188
  232.8 2.6 copy-start.2
  259.8 9.1 %copy-start.9 = (s32[2]{0:T(128)S(1)}, s32[2]{0:T(128)}, u32[]{:S(2)}) copy-start(s32[2]{0:T(128)} %constant.80.clone) | copy-start | bytes 28
  259.9 146.8 %reduce-scatter.8.cloned.1.call-start = ((), (), s32[]{:S(2)}) async-start(), calls=%async_computation.6 | async-start | bytes 589824 | tf_op jit(solution)/shard_map/reduce_scatter | solution.py:139
  282.1 1.5 copy-start.7
  282.1 126.1 %copy-start.1 = (bf16[1,256,6144]{2,1,0:T(8,128)(2,1)S(1)}, bf16[1,256,6144]{2,1,0:T(8,128)(2,1)}, u32[]{:S(2)}) copy-start(bf16[1,256,6144]{2,1,0:T(8,128)(2,1)} %param.28) | copy-start | bytes 9437188
  283.5 79.0 %copy-start.4 = (bf16[1,512,192]{2,1,0:T(8,128)(2,1)S(1)}, bf16[1,512,192]{2,1,0:T(8,128)(2,1)}, u32[]{:S(2)}) copy-start(bf16[1,512,192]{2,1,0:T(8,128)(2,1)} %reduce-scatter.6.cloned.1.call-done) | copy-start | bytes 589828
Sparse Core Ops, SparseCore 0:
  15.5 50.8 all-gather.1
  93.0 41.7 reduce-scatter.5
  260.0 100.6 reduce-scatter.9
  369.6 36.9 reduce-scatter.7
